TPU v7x, 256 devices: a whole 4x4x8 slice. The times are simulated.
256 devices in a mesh: dp: 4 (over y), seq: 8 (over x, core), tensor: 8 (over z).
Axes of the slice: x: 4, y: 4, z: 8, core: 2. Of those that a mesh axis runs over, the one named last changes fastest.
Arguments:
- tokens: bfloat16 [4, 4096, 8192], P('dp', ('seq', 'tensor')), may hold values from -19 to 19
- norm_gain: float32 [8192], replicated, may hold values from 0.1 to 1.9
- master_weight: float32 [8192, 3, 4096], P(('dp', 'seq'), None, 'tensor'), may hold values from -5 to 5
- short_filter: float32 [3, 3, 4096], P(None, None, 'tensor'), may hold values from -2600 to 2600
- medium_filter: bfloat16 [128, 4096], P(None, 'tensor'), may hold values from -1 to 1
- medium_skip: float32 [4096], P('tensor'), may hold values from 0.5 to 1.5
Outputs:
- mixed: bfloat16 [4, 4096, 4096], P('dp', 'seq', 'tensor')
- weight_amax: float32 [1], replicated
All inputs are finite; a program needn't handle non-finite values.
Results may differ from a plain program's by a relative error of at most 0.015.
Values may be sent and summed in bfloat16 or wider, within the bound.
A program may use at most 128 MiB of HBM per device.

v0:
```python
import jax
import jax.numpy as jnp
from jax import lax
from jax.sharding import PartitionSpec as P

grid_top = 448.0
eps_norm = 1e-06
eps_peak = 1e-06
power_steps = [2.0, 4.0, 16.0, 256.0, 65536.0, 4294967296.0, 1.8446744073709552e19]


def passed_along(x, axis, by):
    length = lax.axis_size(axis)
    pairs = [(i, i + by) for i in range(length) if 0 <= i + by < length]
    return lax.ppermute(x, axis, pairs)


def exact_power(exponent):
    magnitude = jnp.abs(exponent)
    result = jnp.ones(exponent.shape, jnp.float32)
    for bit_place in range(7):
        chosen = magnitude >> bit_place & 1 == 1
        result = result * jnp.where(chosen, power_steps[bit_place], 1.0)
    return jnp.where(exponent >= 0, result, 1.0 / result)


def narrow_grid(entries):
    magnitude = jnp.abs(entries)
    exponent = jnp.floor(jnp.log2(jnp.maximum(magnitude, 1e-30))).astype(jnp.int32)
    quantum = exact_power(jnp.maximum(exponent, -6) - 3)
    return jnp.sign(entries) * jnp.floor(magnitude / quantum + 0.5) * quantum


def short_conv(padded, filters, length, margin):
    summed = jnp.zeros((length,) + padded.shape[1:], jnp.float32)
    for lag_index in range(filters.shape[1]):
        window = padded[margin - lag_index : margin - lag_index + length].astype(jnp.float32)
        summed = summed + filters[:, lag_index, :] * window
    return summed


def shards(tokens, norm_gain, master_weight, short_filter, medium_filter, medium_skip):
    short_taps = short_filter.shape[1]
    medium_taps = medium_filter.shape[0]
    values = tokens.astype(jnp.float32)
    square_mean = jnp.mean(values * values, axis=-1, keepdims=True)
    normed = (values * lax.rsqrt(square_mean + eps_norm) * norm_gain).astype(jnp.bfloat16)
    gathered = lax.all_gather(normed, "tensor", axis=1, tiled=True)
    stacks = gathered.shape[0]
    seq_rows = gathered.shape[1]
    model_width = gathered.shape[2]
    flat_rows = gathered.reshape(stacks * seq_rows, model_width)
    owned_rows = master_weight.shape[0]
    channels = master_weight.shape[2]
    peak_value = lax.pmax(jnp.max(jnp.abs(master_weight)), ("dp", "seq", "tensor"))
    factor = exact_power(jnp.floor(jnp.log2(grid_top / (peak_value + eps_peak))).astype(jnp.int32))
    recast = (
        narrow_grid(master_weight * factor).astype(jnp.bfloat16).reshape(owned_rows, 3 * channels)
    )
    projected = jnp.dot(
        flat_rows,
        lax.all_gather(recast, ("dp", "seq"), axis=0, tiled=True),
        preferred_element_type=jnp.float32,
    )
    features = (projected / factor).astype(jnp.bfloat16).reshape(seq_rows, 3, channels)
    rim_rows = passed_along(features[seq_rows - (short_taps - 1) :], "seq", 1)
    padded = jnp.concatenate([rim_rows, features], axis=0)
    mixed_conv = short_conv(padded, short_filter, seq_rows, short_taps - 1)
    gated = (mixed_conv[:, 1] * mixed_conv[:, 2]).astype(jnp.bfloat16)
    earlier = passed_along(gated[seq_rows - (medium_taps - 1) :], "seq", 1)
    extended = jnp.concatenate([earlier, gated], axis=0)
    post_gate = mixed_conv[:, 0]
    kernel = medium_filter[::-1][:, None, :]
    filtered = lax.conv_general_dilated(
        extended[None],
        kernel,
        (1,),
        "VALID",
        dimension_numbers=("NWC", "WIO", "NWC"),
        feature_group_count=channels,
        preferred_element_type=jnp.float32,
    )[0]
    filtered = filtered + medium_skip * gated.astype(jnp.float32)
    mixed_rows = (post_gate * filtered).astype(jnp.bfloat16)
    return (mixed_rows[None], peak_value.reshape(1))


def solution(mesh):
    placed = (
        P("dp", ("seq", "tensor"), None),
        P(),
        P(("dp", "seq"), None, "tensor"),
        P(None, None, "tensor"),
        P(None, "tensor"),
        P("tensor"),
    )
    return jax.shard_map(
        shards,
        mesh=mesh,
        in_specs=placed,
        out_specs=(P("dp", "seq", "tensor"), P()),
        check_vma=False,
    )
```

profile of v0, /device:TPU:1, one launch (start us, length us, event | category | flops | bytes accessed | tf_op | source)
XLA Modules:
  0.0 297.4 jit_solution(4098233784942228399)
XLA Ops:
  7.2 0.0 all-gather.3.cloned.1.call-start
  7.2 1.6 fusion.5
  8.9 0.0 copy-start.1
  8.9 2.2 fusion.7
  11.0 0.0 all-gather.3.cloned.1.call-update
  11.0 0.0 all-gather.5.cloned.1.call-start
  11.1 0.0 copy-done.1
  11.1 0.7 abs_reduce_fusion
  11.8 83.3 %pmax.7 = f32[]{:T(128)} all-reduce(f32[]{:T(128)} %abs_reduce_fusion), channel_id=1, replica_groups=mesh['dp'=4,'seq'=8,'tensor'=8] {'dp','seq','tensor'}, use_global_device_ids=true, to_apply=%region_2.0 | all-reduce | flops 1 | bytes 8 | tf_op jit(solution)/shard_map/pmax | solution.py:55
  95.1 0.5 copy.13
  96.4 0.0 copy-start.4
  96.4 4.1 %multiply_convert_fusion = bf16[256,3,512]{0,2,1:T(8,128)(2,1)} fusion(f32[256,3,512]{0,2,1:T(8,128)S(1)} %copy.13, f32[]{:T(128)S(6)} %select_n.59), kind=kLoop, calls=%fused_computation.14 | loop fusion | flops 20840448 | bytes 2359300 | tf_op jit(solution)/shard_map/convert_element_type | solution.py:58
  100.5 0.0 all-gather.5.cloned.1.call-update
  100.6 10.0 %all-gather.3.cloned.1.call-done = bf16[1,512,8192]{2,1,0:T(8,128)(2,1)} async-done(((bf16[1,64,8192]{2,1,0:T(8,128)(2,1)}), bf16[1,512,8192]{2,1,0:T(8,128)(2,1)}) %all-gather.3.cloned.1.call-update) | async-done | bytes 8388624 | tf_op jit(solution)/shard_map/all_gather | solution.py:48
  110.6 109.6 %all-gather.5.cloned.1.call-done = bf16[8192,1536]{0,1:T(8,128)(2,1)} async-done(((bf16[256,1536]{0,1:T(8,128)(2,1)}), bf16[8192,1536]{0,1:T(8,128)(2,1)}) %all-gather.5.cloned.1.call-update) | async-done | bytes 25165840 | tf_op jit(solution)/shard_map/all_gather | solution.py:62
  220.2 19.4 %divide_convert_fusion = bf16[512,1536]{1,0:T(8,128)(2,1)S(1)} fusion(bf16[8192,1536]{0,1:T(8,128)(2,1)} %all-gather.5.cloned.1.call-done, bf16[1,512,8192]{2,1,0:T(8,128)(2,1)} %all-gather.3.cloned.1.call-done, f32[]{:T(128)S(6)} %select_n.59), kind=kOutput, calls=%fused_computation.3 | convolution fusion | flops 12886474752 | bytes 35127300 | tf_op jit(solution)/shard_map/dot_general | solution.py:60
  239.6 3.2 %collective-permute-start = (bf16[2,3,512]{2,1,0:T(4,128)(2,1)S(1)}, bf16[2,3,512]{2,1,0:T(4,128)(2,1)S(1)}, u32[]{:S(2)}, u32[]{:S(2)}) collective-permute-start(bf16[2,3,512]{2,1,0:T(4,128)(2,1)S(1)} %slice.39), channel_id=1, source_target_pairs={{0,8},{8,16},{16,24},{24,32},{32,40},{40,48},{48,56},{1,9},{9,17},... | collective-permute-start | bytes 18440 | tf_op jit(solution)/shard_map/ppermute | solution.py:15
  242.8 1.6 copy.14
  244.4 3.2 %copy.15 = bf16[512,3,512]{2,1,0:T(4,128)(2,1)S(1)} copy(bf16[512,3,512]{0,2,1:T(8,128)(2,1)} %bitcast.34) | data formatting | bytes 3145728 | tf_op jit(solution)/shard_map/reshape | solution.py:65
  247.6 0.0 collective-permute-done
  247.6 5.1 %multiply_add_fusion = f32[512,3,512]{2,1,0:T(4,128)S(1)} fusion(bf16[512,3,512]{2,1,0:T(4,128)(2,1)S(1)} %copy.15, bf16[2,3,512]{2,1,0:T(4,128)(2,1)S(1)} %collective-permute-done, f32[3,512]{1,0:T(4,128)S(1)} %get-tuple-element.7, f32[3,512]{1,0:T(4,128)S(1)} %get-tuple-element.8, f32[3,512]{1,0:T(4,128)S(1)} %bitcast.39), kind=kLoop, calls=%fused_computation.2 | loop fusion | flops 7864320 | bytes 4743168 | tf_op jit(solution)/shard_map/add | solution.py:38
  252.7 1.9 copy-done
  254.7 1.6 fusion.13
  256.3 0.3 slice.54
  256.6 0.0 copy-start.5
  256.6 2.3 collective-permute-start.1
  259.0 0.2 rev.3
  259.2 0.1 copy.39
  259.3 1.4 collective-permute-done.1
  260.7 0.1 maximum_bitcast_fusion
  260.9 28.8 %fusion.15 = bf16[1,512,512]{2,0,1:T(2,128)(2,1)S(1)} fusion(f32[512,3,512]{2,1,0:T(4,128)} %copy-done, bf16[1,639,512]{2,1,0:T(8,128)(2,1)S(1)} %maximum_bitcast_fusion, bf16[512,1,512]{2,1,0:T(2,128)(2,1)S(1)} %fusion.13, f32[512]{0:T(512)S(1)} %copy-done.5, bf16[128,1,512]{2,0,1:T(8,128)(2,1)S(1)} %bitcast.38), kind=kOutput, calls=%fused_computation.31 | convolution fusion | flops 68419584 | bytes 2884608 | tf_op jit(solution)/shard_map/conv_general_dilated | solution.py:74
  289.7 0.9 copy.20
  (14 shorter events, 0.1 us)
Async XLA Ops:
  7.2 1.7 copy-start.2
  7.2 103.4 %all-gather.3.cloned.1.call-start = ((), (), s32[]{:S(2)}) async-start(), calls=%async_computation | async-start | bytes 9437184 | tf_op jit(solution)/shard_map/all_gather | solution.py:48
  8.9 2.2 copy-start.1
  11.0 209.1 %all-gather.5.cloned.1.call-start = ((), (), s32[]{:S(2)}) async-start(), calls=%async_computation.1 | async-start | bytes 25952256 | tf_op jit(solution)/shard_map/all_gather | solution.py:62
  96.4 4.1 %copy-start.4 = (f32[3,3,512]{2,1,0:T(4,128)S(1)}, f32[3,3,512]{2,1,0:T(4,128)}, u32[]{:S(2)}) copy-start(f32[3,3,512]{2,1,0:T(4,128)} %param.9) | copy-start | bytes 55300
  239.6 8.1 %collective-permute-start = (bf16[2,3,512]{2,1,0:T(4,128)(2,1)S(1)}, bf16[2,3,512]{2,1,0:T(4,128)(2,1)S(1)}, u32[]{:S(2)}, u32[]{:S(2)}) collective-permute-start(bf16[2,3,512]{2,1,0:T(4,128)(2,1)S(1)} %slice.39), channel_id=1, source_target_pairs={{0,8},{8,16},{16,24},{24,32},{32,40},{40,48},{48,56},{1,9},{9,17},... | collective-permute-start | bytes 18440 | tf_op jit(solution)/shard_map/ppermute | solution.py:15
  252.7 1.9 copy-start
  254.7 4.3 %copy-start.3 = (bf16[128,512]{1,0:T(8,128)(2,1)S(1)}, bf16[128,512]{1,0:T(8,128)(2,1)}, u32[]{:S(2)}) copy-start(bf16[128,512]{1,0:T(8,128)(2,1)} %param.10) | copy-start | bytes 393220
  256.6 4.2 %copy-start.5 = (f32[512]{0:T(512)S(1)}, f32[512]{0:T(512)}, u32[]{:S(2)}) copy-start(f32[512]{0:T(512)} %param.11) | copy-start | bytes 6148
  256.6 4.1 %collective-permute-start.1 = (bf16[127,512]{1,0:T(8,128)(2,1)S(1)}, bf16[127,512]{1,0:T(8,128)(2,1)S(1)}, u32[]{:S(2)}, u32[]{:S(2)}) collective-permute-start(bf16[127,512]{1,0:T(8,128)(2,1)S(1)} %bitcast.37), channel_id=1, source_target_pairs={{0,8},{8,16},{16,24},{24,32},{32,40},{40,48},{48,56},{1,9},{9,17},... | collective-permute-start | bytes 390152 | tf_op jit(solution)/shard_map/ppermute | solution.py:15
Sparse Core Ops, SparseCore 0:
  11.2 99.3 all-gather.2
  113.0 107.0 all-gather.4
where the time goes:
time: 298 us; the launch traced here: 297 us
  waiting for transfers between devices  121 us (41%)
  blocking collectives  83.3 us (28%)
  matrix products  48.1 us (16%)
  other arithmetic  15.4 us (5%)
  between operations  15.1 us (5%)
  local copies, waits for them, and re-layouts  8.8 us (3%)
  starting transfers between devices  5.61 us (2%)
    all_gather x1, waiting for transfers between devices, shards(): lax.all_gather(recast, ('dp', 'seq'), axis=0, tiled=True)  110 us
    pmax x1, blocking collectives, shards(): lax.pmax(jnp.max(jnp.abs(master_weight)), ('dp', 'seq', 'tensor'))  83.3 us
    conv_general_dilated x1, matrix products, shards(): lax.conv_general_dilated(extended[None], kernel, (1,), 'VALID', dimension...  28.8 us
    dot_general x1, matrix products, shards(): jnp.dot(flat_rows, lax.all_gather(recast, ('dp', 'seq'), axis=0, tiled=Tr...  19.4 us
    all_gather x1, waiting for transfers between devices, shards(): gathered = lax.all_gather(normed, 'tensor', axis=1, tiled=True)  9.99 us
  transfers between devices with their start and end apart: 4, of which 3 were waited for; matrix products, arithmetic and copies ran while one was open for 4% of the time, Pallas kernels for 0%

commit v1 on v0

v1 whole, which is shorter than its diff:
```python
import functools
import heapq

import jax
import jax.numpy as jnp
import numpy as np
from jax import lax
from jax.experimental import pallas as pl
from jax.experimental.pallas import tpu as pltpu
from jax.sharding import PartitionSpec as P

MESH = pl.DeviceIdType.MESH
F32 = jnp.float32
BF16 = jnp.bfloat16
eps_norm = 1e-06
eps_peak = 1e-06
grid_top = 448.0

ring_slots = [0, 1, -1, 2, -2, 3, -3, 4]
slot_of = {d: s for s, d in enumerate(ring_slots)}
slot_of[-4] = slot_of[4]


def wrap4(d):
    return {-2: 2, 3: -1, -3: 1}.get(d, d)


def plan_messages():
    msgs = {}
    half_block = 32 * 8192 * 2
    for sign, link in ((1, "zp"), (-1, "zm")):
        for i in range(7):
            hop, sub = i // 2, i % 2
            if i == 6:
                sub = 0 if sign == 1 else 1
            dep = []
            if hop > 0:
                dep = [(link, i - 2 if i < 6 else (4 if sign == 1 else 5))]
            msgs[(link, i)] = (link, half_block, dep, ("tok", -sign * hop, sub))
    quarter = 64 * 1536 * 2

    def ring(half, axis, fixed, need):
        first = 2 * half
        for sign in (1, -1):
            link = axis + ("p" if sign == 1 else "m")
            order = (first, first + 1) if sign == 1 else (first + 1, first)
            names = [(half, link, fixed, n) for n in range(3)]
            place = lambda d: (0, d) if axis == "x" else (d, 0)
            spot = lambda d: (fixed, d) if axis == "x" else (d, fixed)
            for n in range(2):
                msgs[names[n]] = (link, quarter, need(order[n]), ("w",) + spot(0) + (order[n],))
            msgs[names[2]] = (link, quarter, [names[0]], ("w",) + spot(-sign) + (order[0],))

    def arrival(half, axis, fixed, d, q):
        first = 2 * half
        if d == 0:
            return []
        if d == 2:
            return [(half, axis + ("p" if q == first else "m"), fixed, 2)]
        sign = -d
        order = (first, first + 1) if sign == 1 else (first + 1, first)
        return [(half, axis + ("p" if sign == 1 else "m"), fixed, order.index(q))]

    ring(0, "x", 0, lambda q: [])
    ring(1, "y", 0, lambda q: [])
    got = {}
    for d in (0, -1, 1, 2):
        for q in (0, 1):
            got[(0, d, q)] = arrival(0, "x", 0, d, q)
        for q in (2, 3):
            got[(d, 0, q)] = arrival(1, "y", 0, d, q)
    second = {}
    for d in (0, -1, 1, 2):
        tag0, tag1 = ("s", d), ("s", d)

        def ring2(half, axis, across):
            first = 2 * half
            for sign in (1, -1):
                link = axis + ("p" if sign == 1 else "m")
                order = (first, first + 1) if sign == 1 else (first + 1, first)
                names = [(half, link, ("s", across), n) for n in range(3)]
                spot = lambda e: (across, e) if axis == "x" else (e, across)
                for n in range(2):
                    key = spot(0) + (order[n],)
                    msgs[names[n]] = (link, quarter, got[key], ("w",) + spot(0) + (order[n],))
                msgs[names[2]] = (link, quarter, [names[0]], ("w",) + spot(-sign) + (order[0],))
            for e in (-1, 1, 2):
                for q in (first, first + 1):
                    if e == 2:
                        name = (half, axis + ("p" if q == first else "m"), ("s", across), 2)
                    else:
                        sign = -e
                        order = (first, first + 1) if sign == 1 else (first + 1, first)
                        name = (half, axis + ("p" if sign == 1 else "m"), ("s", across), order.index(q))
                    second[spot(e) + (q,)] = [name]

        ring2(0, "y", d)
        ring2(1, "x", d)
    got.update(second)
    for dy in (0, -1, 1, 2):
        for dx in (0, -1, 1, 2):
            for h in (0, 1):
                need = got[(dy, dx, 2 * h)] + got[(dy, dx, 2 * h + 1)]
                msgs[("pair", dy, dx, h)] = ("core", 2 * quarter, need, ("half", dy, dx, h))
    return msgs, got


def timeline(msgs):
    rate = {"z": 46.0e3, "x": 46.0e3, "y": 46.0e3, "c": 250.0e3}
    children = {}
    for name, (_, _, need, _) in msgs.items():
        for dep in need:
            children.setdefault(dep, []).append(name)
    rank = {name: i for i, name in enumerate(msgs)}
    left = {name: len(need) for name, (_, _, need, _) in msgs.items()}
    ready = {}
    heap = []
    for name, (link, _, need, _) in msgs.items():
        if not need:
            ready[name] = 4.0 if link[0] == "z" else 15.0
            heapq.heappush(heap, (ready[name], rank[name], name))
    free, arrive, issue = {}, {}, {}
    while heap:
        at, _, name = heapq.heappop(heap)
        link, size, _, _ = msgs[name]
        start = max(at, free.get(link, 0.0))
        free[link] = start + size / rate[link[0]]
        issue[name] = at
        arrive[name] = free[link] + 1.5
        for child in children.get(name, ()):
            left[child] -= 1
            ready[child] = max(ready.get(child, 0.0), arrive[name])
            if left[child] == 0:
                heapq.heappush(heap, (ready[child], rank[child], child))
    return issue, arrive


def plan():
    msgs, got = plan_messages()
    issue, arrive = timeline(msgs)
    tok_need = {0: []}
    for sign, link in ((1, "zp"), (-1, "zm")):
        for hop in range(3):
            tok_need[-sign * (hop + 1)] = [(link, 2 * hop), (link, 2 * hop + 1)]
    tok_need[4] = [("zp", 6), ("zm", 6)]
    row_need = {}
    for dy in (0, -1, 1, 2):
        need = []
        for dx in (0, -1, 1, 2):
            for q in range(4):
                need += got[(dy, dx, q)]
            need += [("pair", dy, dx, h) for h in (0, 1)]
        row_need[dy] = need
    near = sum((tok_need[d] for d in (0, 1, -1, 2, -2)), [])
    mid = sum((tok_need[d] for d in (3, -3)), [])
    far = tok_need[4]
    tasks = [
        (near + row_need[0], 0, 320, 0),
        (near + row_need[-1], 0, 320, -1),
        (near + row_need[1], 0, 320, 1),
        (mid + row_need[0], 320, 448, 0),
        (mid + row_need[-1], 320, 448, -1),
        (mid + row_need[1], 320, 448, 1),
        (near + mid + row_need[2], 0, 448, 2),
        (far, 448, 512, None),
    ]
    events = [(issue[name], 0, i, ("send", name)) for i, name in enumerate(msgs)]
    for i, (need, lo, hi, dy) in enumerate(tasks):
        at = max(arrive[n] for n in need)
        if i and at < last:
            at = last
        last = at + 0.01
        events.append((at, 1, i, ("dot", need, lo, hi, dy)))
    events.sort(key=lambda e: e[:3])
    return msgs, [e[3] for e in events], max(arrive.values())


def dft_tables():
    n = np.arange(256)
    k = np.arange(128)[:, None]
    angle = 2.0 * np.pi * ((k * n[None, :]) % 256) / 256.0
    lower = np.sin(angle)
    lower[0] = np.cos(np.pi * n)
    full = np.concatenate([np.cos(angle), lower], axis=0)

    def split(a):
        a = a.astype(np.float32)
        hi = a.astype(BF16)
        lo = (a - hi.astype(np.float32)).astype(BF16)
        return np.stack([hi, lo])

    return split(full), split(full[:, 128:].T)


def round_grid(v):
    m = jnp.abs(v)
    t = m * F32(8388609.0)
    top = t - t * F32(1.0 - 2.0**-24)
    quantum = jnp.maximum(top, F32(2.0**-6)) * F32(0.125)
    magic = quantum * F32(1.5 * 2.0**23)
    r = (m + magic) - magic
    r = jnp.where(m - r == quantum * F32(0.5), r + quantum, r)
    return jnp.where(v < 0, -r, r)


def kernel(
    program,
    tok_hbm, gain_hbm, w_hbm, sf_hbm, mf_hbm, skip_hbm, f_hbm, g_hbm,
    out_ref, peak_ref,
    tok_in, gain, w_in, sf, mf, skip, fmat, gmat,
    a_all, w_all, acc, feat, gext, hspec, peaks,
    local_sem, send_sem, recv_sem, pk_send, pk_recv, halo_send, halo_recv,
):
    msgs, events, ids = program
    y = lax.axis_index("dp")
    s = lax.axis_index("seq")
    z = lax.axis_index("tensor")
    x, c = s // 2, s % 2

    ins = [(w_hbm, w_in), (tok_hbm, tok_in), (gain_hbm, gain), (mf_hbm, mf), (f_hbm, fmat), (g_hbm, gmat), (sf_hbm, sf), (skip_hbm, skip)]
    loads = [pltpu.make_async_copy(src, dst, local_sem.at[i]) for i, (src, dst) in enumerate(ins)]
    for load in loads:
        load.start()

    def dev(dy, ds, dz):
        return ((y + dy) % 4, ds, (z + dz) % 8)

    barrier = pltpu.get_barrier_semaphore()
    peers = [dev(0, s, k) for k in range(1, 8)] + [dev(0, (s + k) % 8, 0) for k in range(1, 8)] + [dev(k, s, 0) for k in range(1, 4)]
    for peer in peers:
        pl.semaphore_signal(barrier, inc=1, device_id=peer, device_id_type=MESH)

    loads[0].wait()
    top = jnp.zeros((8, 512), F32)
    part = [jnp.zeros((8, 512), F32) for _ in range(4)]
    for k in range(3):
        for r in range(0, 256, 32):
            for j in range(4):
                part[j] = jnp.maximum(part[j], jnp.abs(w_in[k, r + 8 * j : r + 8 * j + 8, :]))
    top = jnp.maximum(jnp.maximum(part[0], part[1]), jnp.maximum(part[2], part[3]))
    top = jnp.max(jnp.max(top, axis=0, keepdims=True), axis=1, keepdims=True)
    peaks[0] = jnp.broadcast_to(top, (8, 128))

    def norm_rows(lo):
        for r in range(lo, lo + 32, 16):
            v = tok_in[r : r + 16, :].astype(F32)
            mean = jnp.sum(v * v, axis=1, keepdims=True) * F32(1.0 / 8192)
            a_all[r : r + 16, :] = (v * lax.rsqrt(mean + F32(eps_norm)) * gain[...]).astype(BF16)

    loads[1].wait()
    loads[2].wait()
    norm_rows(0)

    def peak_round(src, base, targets):
        copies = []
        for i, target in enumerate(targets):
            copies.append(
                pltpu.make_async_remote_copy(
                    src_ref=peaks.at[src], dst_ref=peaks.at[3 + base + i],
                    send_sem=pk_send.at[base + i], recv_sem=pk_recv.at[base + i],
                    device_id=target, device_id_type=MESH,
                )
            )
        for copy in copies:
            copy.start()
        return copies

    def peak_finish(copies, src, base):
        best = peaks[src]
        for i, copy in enumerate(copies):
            copy.wait_recv()
            best = jnp.maximum(best, peaks[3 + base + i])
        return best

    def w_row(dy, dx, parity):
        return (((y + dy) % 4) * 8 + ((x + dx) % 4) * 2 + parity) * 256

    def message(name):
        link, _, _, place = msgs[name]
        if place[0] == "tok":
            _, d, sub = place
            step = 1 if link == "zp" else -1
            here = slot_of[d] * 64 + 32 * sub
            there = slot_of[d - step] * 64 + 32 * sub
            src, dst = a_all.at[here : here + 32, :], a_all.at[there : there + 32, :]
            target = dev(0, s, step)
        elif place[0] == "w":
            _, dy, dx, q = place
            row = pl.multiple_of(w_row(dy, dx, c) + 64 * q, 64)
            src = dst = w_all.at[pl.ds(row, 64), :]
            if link[0] == "x":
                target = dev(0, (s + (2 if link[1] == "p" else 6)) % 8, 0)
            else:
                target = dev(1 if link[1] == "p" else 3, s, 0)
        else:
            _, dy, dx, h = place
            row = pl.multiple_of(w_row(dy, dx, c) + 128 * h, 128)
            src = dst = w_all.at[pl.ds(row, 128), :]
            target = (y, x * 2 + 1 - c, z)
        i = ids[name]
        return pltpu.make_async_remote_copy(
            src_ref=src, dst_ref=dst, send_sem=send_sem.at[i], recv_sem=recv_sem.at[i], device_id=target, device_id_type=MESH
        )

    copies = {name: message(name) for name in msgs}
    arrived = set()

    def need(names):
        for name in names:
            if name not in arrived:
                arrived.add(name)
                copies[name].wait_recv()

    pl.semaphore_wait(barrier, len(peers))
    round0 = peak_round(0, 0, peers[:7])
    copies[("zp", 0)].start()
    copies[("zm", 0)].start()
    norm_rows(32)
    copies[("zp", 1)].start()
    copies[("zm", 1)].start()
    peaks[1] = peak_finish(round0, 0, 0)
    round1 = peak_round(1, 7, peers[7:14])
    peaks[2] = peak_finish(round1, 1, 7)
    round2 = peak_round(2, 14, peers[14:])
    peak = peak_finish(round2, 2, 14)
    peak_ref[0] = jnp.max(peak)

    ratio = F32(grid_top) / (peak + F32(eps_peak))
    factor = jnp.ones((8, 128), F32)
    inverse = jnp.ones((8, 128), F32)
    for p in (16, 8, 4, 2, 1):
        larger = factor * F32(2.0**p)
        over = ratio >= larger
        factor = jnp.where(over, larger, factor)
        inverse = jnp.where(over, inverse * F32(2.0**-p), inverse)
    factor = jnp.broadcast_to(factor[0:1, 0:1], (1, 512))
    inverse = jnp.broadcast_to(inverse[0:1, 0:1], (1, 512))
    own = pl.multiple_of(w_row(0, 0, c), 256)
    started = {("zp", 0), ("zm", 0), ("zp", 1), ("zm", 1)}

    def recast(i, carry):
        r = pl.multiple_of(i * 32, 32)
        for k in range(3):
            w_all[pl.ds(own + r, 32), 512 * k : 512 * k + 512] = round_grid(w_in[k, pl.ds(r, 32), :] * factor).astype(BF16)
        return carry

    lax.fori_loop(0, 8, recast, 0)

    def spectrum():
        for load in loads[3:]:
            load.wait()
        taps = mf[...]
        h = jnp.dot(fmat[0, :, 0:128], taps, preferred_element_type=F32) + jnp.dot(fmat[1, :, 0:128], taps, preferred_element_type=F32)
        first = lax.broadcasted_iota(jnp.int32, (128, 512), 0) == 0
        scale = jnp.where(first, F32(1.0 / 256), F32(2.0 / 256))
        hc, hs = h[0:128] * scale, h[128:256] * scale
        hspec[0] = hc
        hspec[1] = jnp.where(first, F32(0.0), hs)
        hspec[2] = jnp.where(first, hs, hc)

    def product(lo, hi, dy, fresh):
        rows = hi - lo
        if dy is None:
            k0, depth = 0, 8192
        else:
            k0, depth = pl.multiple_of(((y + dy) % 4) * 2048, 2048), 2048

        def column(i, carry):
            n = pl.multiple_of(i * 512, 512)
            left = a_all[lo:hi, :] if dy is None else a_all[lo:hi, pl.ds(k0, depth)]
            got = jnp.dot(left, w_all[pl.ds(k0, depth), pl.ds(n, 512)], preferred_element_type=F32)
            if fresh:
                acc[lo:hi, pl.ds(n, 512)] = got
            else:
                acc[lo:hi, pl.ds(n, 512)] += got
            return carry

        lax.fori_loop(0, 3, column, 0)

    touched = set()
    ready = False
    for event in events:
        if event[0] == "send":
            name = event[1]
            if name in started:
                continue
            need(msgs[name][2])
            copies[name].start()
            if not ready and msgs[name][2]:
                ready = True
                spectrum()
        else:
            _, names, lo, hi, dy = event
            need(names)
            product(lo, hi, dy, lo not in touched)
            touched.add(lo)
            if hi == 448 and lo == 0:
                touched.add(320)

    inverse_row = inverse
    for slot, d in enumerate(ring_slots):
        row = pl.multiple_of(8 + 64 * ((z + d) % 8), 8)
        for k in range(3):
            cols = slice(512 * k, 512 * k + 512)
            feat[pl.ds(row, 64), cols] = (acc[64 * slot : 64 * slot + 64, cols] * inverse_row).astype(BF16).astype(F32)

    after = (y, (s + 1) % 8, z)
    rim = pltpu.make_async_remote_copy(
        src_ref=feat.at[512:520, :], dst_ref=feat.at[0:8, :], send_sem=halo_send.at[0], recv_sem=halo_recv.at[0],
        device_id=after, device_id_type=MESH,
    )
    rim.start()

    def short(k, lo, rows):
        total = jnp.zeros((rows, 512), F32)
        for j in range(3):
            total = total + sf[k, j : j + 1, :] * feat[8 + lo - j : 8 + lo - j + rows, 512 * k : 512 * k + 512]
        return total

    def gate(lo, rows):
        gext[128 + lo : 128 + lo + rows, :] = (short(1, lo, rows) * short(2, lo, rows)).astype(BF16)

    gate(384, 128)
    edge = pltpu.make_async_remote_copy(
        src_ref=gext.at[512:640, :], dst_ref=gext.at[0:128, :], send_sem=halo_send.at[1], recv_sem=halo_recv.at[1],
        device_id=after, device_id_type=MESH,
    )
    edge.start()
    gate(256, 128)
    gate(128, 128)
    gate(16, 112)

    def mix(b):
        lo = 128 * b
        e = gext[lo : lo + 256, :]
        t = jnp.dot(fmat[0], e, preferred_element_type=F32) + jnp.dot(fmat[1], e, preferred_element_type=F32)
        tc, ts = t[0:128], t[128:256]
        pc = tc * hspec[0] - ts * hspec[1]
        ps = tc * hspec[1] + ts * hspec[2]
        p = jnp.concatenate([pc, ps], axis=0)
        ph = p.astype(BF16)
        pl_ = (p - ph.astype(F32)).astype(BF16)
        f = jnp.dot(gmat[0], ph, preferred_element_type=F32)
        f = f + jnp.dot(gmat[0], pl_, preferred_element_type=F32)
        f = f + jnp.dot(gmat[1], ph, preferred_element_type=F32)
        f = f + skip[...] * e[128:256].astype(F32)
        out_ref[lo : lo + 128, :] = (short(0, lo, 128) * f).astype(BF16)

    mix(3)
    mix(2)
    rim.wait_recv()
    edge.wait_recv()

    @pl.when(s == 0)
    def _():
        feat[0:8, :] = jnp.zeros((8, 1536), F32)
        gext[0:128, :] = jnp.zeros((128, 512), BF16)

    gate(0, 16)
    mix(1)
    mix(0)
    rim.wait_send()
    edge.wait_send()
    for copy in round0 + round1 + round2:
        copy.wait_send()
    for copy in copies.values():
        copy.wait_send()


def shards(tokens, norm_gain, master_weight, short_filter, medium_filter, medium_skip):
    msgs, events, _ = plan()
    ids = {name: i for i, name in enumerate(msgs)}
    ftab, gtab = dft_tables()
    count = len(msgs)
    any_space = pl.BlockSpec(memory_space=pl.ANY)
    mixed, peak = pl.pallas_call(
        functools.partial(kernel, (msgs, events, ids)),
        out_shape=(jax.ShapeDtypeStruct((512, 512), BF16), jax.ShapeDtypeStruct((1,), F32)),
        in_specs=[any_space] * 8,
        out_specs=(pl.BlockSpec(memory_space=pltpu.VMEM), pl.BlockSpec(memory_space=pltpu.SMEM)),
        scratch_shapes=[
            pltpu.VMEM((64, 8192), BF16),
            pltpu.VMEM((1, 8192), F32),
            pltpu.VMEM((3, 256, 512), F32),
            pltpu.VMEM((3, 3, 512), F32),
            pltpu.VMEM((128, 512), BF16),
            pltpu.VMEM((1, 512), F32),
            pltpu.VMEM((2, 256, 256), BF16),
            pltpu.VMEM((2, 128, 256), BF16),
            pltpu.VMEM((512, 8192), BF16),
            pltpu.VMEM((8192, 1536), BF16),
            pltpu.VMEM((512, 1536), F32),
            pltpu.VMEM((520, 1536), F32),
            pltpu.VMEM((640, 512), BF16),
            pltpu.VMEM((3, 128, 512), F32),
            pltpu.VMEM((20, 8, 128), F32),
            pltpu.SemaphoreType.DMA((8,)),
            pltpu.SemaphoreType.DMA((count,)),
            pltpu.SemaphoreType.DMA((count,)),
            pltpu.SemaphoreType.DMA((17,)),
            pltpu.SemaphoreType.DMA((17,)),
            pltpu.SemaphoreType.DMA((2,)),
            pltpu.SemaphoreType.DMA((2,)),
        ],
        compiler_params=pltpu.CompilerParams(collective_id=0, has_side_effects=True, vmem_limit_bytes=60 * 1024 * 1024),
    )(
        tokens.reshape(64, 8192),
        norm_gain.reshape(1, 8192),
        jnp.transpose(master_weight, (1, 0, 2)),
        short_filter,
        medium_filter,
        medium_skip.reshape(1, 512),
        jnp.asarray(ftab),
        jnp.asarray(gtab),
    )
    return mixed[None], peak


def solution(mesh):
    placed = (
        P("dp", ("seq", "tensor"), None),
        P(),
        P(("dp", "seq"), None, "tensor"),
        P(None, None, "tensor"),
        P(None, "tensor"),
        P("tensor"),
    )
    return jax.shard_map(
        shards,
        mesh=mesh,
        in_specs=placed,
        out_specs=(P("dp", "seq", "tensor"), P()),
        check_vma=False,
    )
```

time: 298 us -> 116 us (0.39)
  waiting for transfers between devices: 121 us -> 0 us
  Pallas kernels: 0 us -> 110 us
  blocking collectives: 83.3 us -> 0 us
  matrix products: 48.1 us -> 0 us
  other arithmetic: 15.4 us -> 0 us
  between operations: 15.1 us -> 2.34 us
  local copies, waits for them, and re-layouts: 8.8 us -> 1.87 us
  starting transfers between devices: 5.61 us -> 0 us
    all_gather x2 -> x0, waiting for transfers between devices: 120 us -> none  [the longest x1 110 us: shards(): lax.all_gather(recast, ('dp', 'seq'), axis=0, tiled=True)]
    pallas_call x0 -> x1, Pallas kernels: none -> 110 us  [shards(): pl.pallas_call(functools.partial(kernel, (msgs, events, ids)), out_shape=...]
    pmax x1 -> x0, blocking collectives: 83.3 us -> none  [shards(): lax.pmax(jnp.max(jnp.abs(master_weight)), ('dp', 'seq', 'tensor'))]
    conv_general_dilated x1 -> x0, matrix products: 28.8 us -> none  [shards(): lax.conv_general_dilated(extended[None], kernel, (1,), 'VALID', dimension...]
    dot_general x1 -> x0, matrix products: 19.4 us -> none  [shards(): jnp.dot(flat_rows, lax.all_gather(recast, ('dp', 'seq'), axis=0, tiled=Tr...]
    convert_element_type x3 -> x0, other arithmetic: 7.88 us -> none  [the longest x1 4.08 us: shards(): narrow_grid(master_weight * factor).astype(jnp.bfloat16)]
    ppermute x2 -> x0, starting transfers between devices: 5.53 us -> none  [passed_along(): return lax.ppermute(x, axis, pairs)]
    add x1 -> x0, other arithmetic: 5.07 us -> none  [short_conv(): summed = summed + filters[:, lag_index, :] * window]
  transfers between devices with their start and end apart: 4 -> 0, of which waited for: 3 -> 0; matrix products, arithmetic and copies ran while one was open for 4% -> 0% of each run, Pallas kernels for 0% -> 0%
where the time goes in v1:
time: 116 us; the launch traced here: 114 us
  Pallas kernels  110 us (95%)
  between operations  2.34 us (2%)
  local copies, waits for them, and re-layouts  1.87 us (2%)
    pallas_call x1, Pallas kernels, shards(): pl.pallas_call(functools.partial(kernel, (msgs, events, ids)), out_shape=...  110 us

profile of v1, /device:TPU:1, one launch (start us, length us, event | category | flops | bytes accessed | tf_op | source)
XLA Modules:
  0.0 114.1 jit_solution(3741206219930521557)
XLA Ops:
  0.6 109.9 %shard_map.95 = (bf16[512,512]{1,0:T(8,128)(2,1)}, f32[1]{0:T(128)}) custom-call(bf16[64,8192]{1,0:T(8,128)(2,1)} %bitcast.6, f32[1,8192]{1,0:T(1,128)} %bitcast.8, f32[3,256,512]{2,1,0:T(8,128)} %bitcast.5, f32[3,3,512]{2,1,0:T(4,128)} %sf_hbm.1, bf16[128,512]{1,0:T(8,128)(2,1)} %mf_hbm.1, f32[1,512]{1,0:T(1,128)} %bitcast.9, ...), custom_call_target="tpu_custom_call" | custom-call | tf_op jit(solution)/shard_map/pallas_call | solution.py:476
  110.5 1.9 %copy.12 = bf16[1,512,512]{2,1,0:T(8,128)(2,1)} copy(bf16[1,512,512]{2,1,0:T(8,128)(2,1)} %bitcast.7) | data formatting | bytes 1048576

commit v2 on v1

--- a/solution.py
+++ b/solution.py
@@ -20,6 +20,8 @@
 slot_of = {d: s for s, d in enumerate(ring_slots)}
 slot_of[-4] = slot_of[4]
 
+chunks = [(0, None), (-1, None), (1, None), (2, 0), (2, -1), (2, 1), (2, 2)]
+
 
 def wrap4(d):
     return {-2: 2, 3: -1, -3: 1}.get(d, d)
@@ -27,16 +29,13 @@
 
 def plan_messages():
     msgs = {}
-    half_block = 32 * 8192 * 2
-    for sign, link in ((1, "zp"), (-1, "zm")):
-        for i in range(7):
-            hop, sub = i // 2, i % 2
-            if i == 6:
-                sub = 0 if sign == 1 else 1
-            dep = []
-            if hop > 0:
-                dep = [(link, i - 2 if i < 6 else (4 if sign == 1 else 5))]
-            msgs[(link, i)] = (link, half_block, dep, ("tok", -sign * hop, sub))
+    for ci, (dy, dx) in enumerate(chunks):
+        size = 64 * 2 * (2048 if dx is None else 512)
+        for sign, link in ((1, "zp"), (-1, "zm")):
+            for hop in range(4):
+                dep = [(link, ci, hop - 1)] if hop else []
+                sub = None if hop < 3 else (0 if sign == 1 else 1)
+                msgs[(link, ci, hop)] = (link, size if hop < 3 else size // 2, dep, ("tok", -sign * hop, sub, ci))
     quarter = 64 * 1536 * 2
 
     def ring(half, axis, fixed, need):
@@ -105,6 +104,22 @@
     return msgs, got
 
 
+def urgency(name):
+    if name[0] in ("zp", "zm"):
+        _, ci, hop = name
+        at = (0.0, 4.0, 8.0, 12.0, 13.0, 14.0, 15.0)[ci]
+        return at + 2.0 * hop if hop or ci > 2 else ci - 10.0
+    if name[0] == "pair":
+        return 0.0
+    half, _, across, n = name
+    if not isinstance(across, tuple):
+        return n * 0.1
+    d = {0: 0, -1: 1, 1: 2, 2: 3}[across[1]]
+    if half == 0:
+        return 10.0 + d * 0.1 + (10.0 if n == 2 else 0.0)
+    return 10.0 + 4.0 * d + n * 0.1
+
+
 def timeline(msgs):
     rate = {"z": 46.0e3, "x": 46.0e3, "y": 46.0e3, "c": 250.0e3}
     children = {}
@@ -113,66 +128,75 @@
             children.setdefault(dep, []).append(name)
     rank = {name: i for i, name in enumerate(msgs)}
     left = {name: len(need) for name, (_, _, need, _) in msgs.items()}
-    ready = {}
+    ready = {name: 0.0 for name in msgs}
+    queue = {link: [] for link in ("zp", "zm", "xp", "xm", "yp", "ym", "core")}
     heap = []
     for name, (link, _, need, _) in msgs.items():
         if not need:
-            ready[name] = 4.0 if link[0] == "z" else 15.0
-            heapq.heappush(heap, (ready[name], rank[name], name))
-    free, arrive, issue = {}, {}, {}
-    while heap:
-        at, _, name = heapq.heappop(heap)
-        link, size, _, _ = msgs[name]
-        start = max(at, free.get(link, 0.0))
-        free[link] = start + size / rate[link[0]]
-        issue[name] = at
-        arrive[name] = free[link] + 1.5
+            ready[name] = 5.0 if link[0] == "z" else 15.0
+            heapq.heappush(heap, (ready[name], 0, rank[name], name))
+    busy = set()
+    arrive, issue = {}, {}
+
+    def serve(link, now):
+        if link in busy or not queue[link]:
+            return
+        _, _, name = heapq.heappop(queue[link])
+        busy.add(link)
+        done = now + msgs[name][1] / rate[link[0]]
+        arrive[name] = done + 1.5
+        issue[name] = now
+        heapq.heappush(heap, (done, 1, rank[name], name))
         for child in children.get(name, ()):
             left[child] -= 1
-            ready[child] = max(ready.get(child, 0.0), arrive[name])
+            ready[child] = max(ready[child], arrive[name])
             if left[child] == 0:
-                heapq.heappush(heap, (ready[child], rank[child], child))
-    return issue, arrive
+                heapq.heappush(heap, (ready[child], 0, rank[child], child))
+
+    while heap:
+        now, kind, _, name = heapq.heappop(heap)
+        link = msgs[name][0]
+        if kind == 1:
+            busy.discard(link)
+        else:
+            heapq.heappush(queue[link], (urgency(name), rank[name], name))
+        if not heap or heap[0][0] > now:
+            for key in queue:
+                serve(key, now)
+    lead = 3.0
+    early = {name: max(ready[name], issue[name] - lead) for name in msgs}
+    return early, arrive
 
 
 def plan():
     msgs, got = plan_messages()
     issue, arrive = timeline(msgs)
-    tok_need = {0: []}
-    for sign, link in ((1, "zp"), (-1, "zm")):
-        for hop in range(3):
-            tok_need[-sign * (hop + 1)] = [(link, 2 * hop), (link, 2 * hop + 1)]
-    tok_need[4] = [("zp", 6), ("zm", 6)]
-    row_need = {}
+    tok_need = {}
+    for ci, (dy, dx) in enumerate(chunks):
+        tok_need[(dy, dx)] = [(link, ci, hop) for link in ("zp", "zm") for hop in range(4)]
+    tasks = []
     for dy in (0, -1, 1, 2):
-        need = []
         for dx in (0, -1, 1, 2):
+            need = list(tok_need[(dy, None)] if (dy, None) in tok_need else tok_need[(dy, dx)])
             for q in range(4):
                 need += got[(dy, dx, q)]
             need += [("pair", dy, dx, h) for h in (0, 1)]
-        row_need[dy] = need
-    near = sum((tok_need[d] for d in (0, 1, -1, 2, -2)), [])
-    mid = sum((tok_need[d] for d in (3, -3)), [])
-    far = tok_need[4]
-    tasks = [
-        (near + row_need[0], 0, 320, 0),
-        (near + row_need[-1], 0, 320, -1),
-        (near + row_need[1], 0, 320, 1),
-        (mid + row_need[0], 320, 448, 0),
-        (mid + row_need[-1], 320, 448, -1),
-        (mid + row_need[1], 320, 448, 1),
-        (near + mid + row_need[2], 0, 448, 2),
-        (far, 448, 512, None),
-    ]
+            tasks.append((max(arrive[n] for n in need), need, dy, dx))
+    tasks.sort(key=lambda t: t[0])
     events = [(issue[name], 0, i, ("send", name)) for i, name in enumerate(msgs)]
-    for i, (need, lo, hi, dy) in enumerate(tasks):
-        at = max(arrive[n] for n in need)
-        if i and at < last:
-            at = last
-        last = at + 0.01
-        events.append((at, 1, i, ("dot", need, lo, hi, dy)))
+    at = 0.0
+    for i, (when, need, dy, dx) in enumerate(tasks):
+        at = max(at, when)
+        events.append((at, 1, i, ("dot", need, dy, dx)))
+        at += 1.3
     events.sort(key=lambda e: e[:3])
-    return msgs, [e[3] for e in events], max(arrive.values())
+    placed, order = set(), []
+    for event in events:
+        if event[3][0] == "send":
+            assert all(dep in placed for dep in msgs[event[3][1]][2])
+            placed.add(event[3][1])
+        order.append(event[3])
+    return msgs, order, at
 
 
 def dft_tables():
@@ -250,6 +274,7 @@
     loads[1].wait()
     loads[2].wait()
     norm_rows(0)
+    norm_rows(32)
 
     def peak_round(src, base, targets):
         copies = []
@@ -278,11 +303,17 @@
     def message(name):
         link, _, _, place = msgs[name]
         if place[0] == "tok":
-            _, d, sub = place
+            _, d, sub, ci = place
             step = 1 if link == "zp" else -1
-            here = slot_of[d] * 64 + 32 * sub
-            there = slot_of[d - step] * 64 + 32 * sub
-            src, dst = a_all.at[here : here + 32, :], a_all.at[there : there + 32, :]
+            off, rows = (0, 64) if sub is None else (32 * sub, 32)
+            here = slot_of[d] * 64 + off
+            there = slot_of[d - step] * 64 + off
+            dy, dx = chunks[ci]
+            if dx is None:
+                cols = pl.ds(pl.multiple_of(((y + dy) % 4) * 2048, 2048), 2048)
+            else:
+                cols = pl.ds(pl.multiple_of(w_row(dy, dx, 0), 512), 512)
+            src, dst = a_all.at[here : here + rows, cols], a_all.at[there : there + rows, cols]
             target = dev(0, s, step)
         elif place[0] == "w":
             _, dy, dx, q = place
@@ -304,6 +335,7 @@
 
     copies = {name: message(name) for name in msgs}
     arrived = set()
+    started = [(link, ci, 0) for ci in range(3) for link in ("zp", "zm")]
 
     def need(names):
         for name in names:
@@ -313,11 +345,8 @@
 
     pl.semaphore_wait(barrier, len(peers))
     round0 = peak_round(0, 0, peers[:7])
-    copies[("zp", 0)].start()
-    copies[("zm", 0)].start()
-    norm_rows(32)
-    copies[("zp", 1)].start()
-    copies[("zm", 1)].start()
+    for name in started:
+        copies[name].start()
     peaks[1] = peak_finish(round0, 0, 0)
     round1 = peak_round(1, 7, peers[7:14])
     peaks[2] = peak_finish(round1, 1, 7)
@@ -336,7 +365,6 @@
     factor = jnp.broadcast_to(factor[0:1, 0:1], (1, 512))
     inverse = jnp.broadcast_to(inverse[0:1, 0:1], (1, 512))
     own = pl.multiple_of(w_row(0, 0, c), 256)
-    started = {("zp", 0), ("zm", 0), ("zp", 1), ("zm", 1)}
 
     def recast(i, carry):
         r = pl.multiple_of(i * 32, 32)
@@ -358,26 +386,21 @@
         hspec[1] = jnp.where(first, F32(0.0), hs)
         hspec[2] = jnp.where(first, hs, hc)
 
-    def product(lo, hi, dy, fresh):
-        rows = hi - lo
-        if dy is None:
-            k0, depth = 0, 8192
-        else:
-            k0, depth = pl.multiple_of(((y + dy) % 4) * 2048, 2048), 2048
+    def product(dy, dx, fresh):
+        k0 = pl.multiple_of(w_row(dy, dx, 0), 512)
 
         def column(i, carry):
             n = pl.multiple_of(i * 512, 512)
-            left = a_all[lo:hi, :] if dy is None else a_all[lo:hi, pl.ds(k0, depth)]
-            got = jnp.dot(left, w_all[pl.ds(k0, depth), pl.ds(n, 512)], preferred_element_type=F32)
+            got = jnp.dot(a_all[:, pl.ds(k0, 512)], w_all[pl.ds(k0, 512), pl.ds(n, 512)], preferred_element_type=F32)
             if fresh:
-                acc[lo:hi, pl.ds(n, 512)] = got
+                acc[:, pl.ds(n, 512)] = got
             else:
-                acc[lo:hi, pl.ds(n, 512)] += got
+                acc[:, pl.ds(n, 512)] += got
             return carry
 
         lax.fori_loop(0, 3, column, 0)
 
-    touched = set()
+    fresh = True
     ready = False
     for event in events:
         if event[0] == "send":
@@ -390,12 +413,10 @@
                 ready = True
                 spectrum()
         else:
-            _, names, lo, hi, dy = event
+            _, names, dy, dx = event
             need(names)
-            product(lo, hi, dy, lo not in touched)
-            touched.add(lo)
-            if hi == 448 and lo == 0:
-                touched.add(320)
+            product(dy, dx, fresh)
+            fresh = False
 
     inverse_row = inverse
     for slot, d in enumerate(ring_slots):

time: 116 us -> 109 us (0.940); the launches traced: 114 us -> 109 us
  Pallas kernels: 110 us -> 105 us
    pallas_call x1, Pallas kernels: 110 us -> 105 us  [shards(): pl.pallas_call(functools.partial(kernel, (msgs, events, ids)), out_shape=...]
where the time goes in v2:
time: 109 us
  Pallas kernels  105 us (96%)
  between operations  2.34 us (2%)
  local copies, waits for them, and re-layouts  1.87 us (2%)
    pallas_call x1, Pallas kernels, shards(): pl.pallas_call(functools.partial(kernel, (msgs, events, ids)), out_shape=...  105 us

profile of v2, /device:TPU:1, one launch (start us, length us, event | category | flops | bytes accessed | tf_op | source)
XLA Modules:
  0.0 109.3 jit_solution(8118262559614525084)
XLA Ops:
  0.6 105.1 %shard_map.95 = (bf16[512,512]{1,0:T(8,128)(2,1)}, f32[1]{0:T(128)}) custom-call(bf16[64,8192]{1,0:T(8,128)(2,1)} %bitcast.6, f32[1,8192]{1,0:T(1,128)} %bitcast.8, f32[3,256,512]{2,1,0:T(8,128)} %bitcast.5, f32[3,3,512]{2,1,0:T(4,128)} %sf_hbm.1, bf16[128,512]{1,0:T(8,128)(2,1)} %mf_hbm.1, f32[1,512]{1,0:T(1,128)} %bitcast.9, ...), custom_call_target="tpu_custom_call" | custom-call | tf_op jit(solution)/shard_map/pallas_call | solution.py:497
  105.7 1.9 %copy.12 = bf16[1,512,512]{2,1,0:T(8,128)(2,1)} copy(bf16[1,512,512]{2,1,0:T(8,128)(2,1)} %bitcast.7) | data formatting | bytes 1048576

commit v3 on v2

--- a/solution.py
+++ b/solution.py
@@ -133,7 +133,7 @@
     heap = []
     for name, (link, _, need, _) in msgs.items():
         if not need:
-            ready[name] = 5.0 if link[0] == "z" else 15.0
+            ready[name] = 4.0 if link[0] == "z" else 14.0
             heapq.heappush(heap, (ready[name], 0, rank[name], name))
     busy = set()
     arrive, issue = {}, {}
@@ -163,7 +163,7 @@
         if not heap or heap[0][0] > now:
             for key in queue:
                 serve(key, now)
-    lead = 3.0
+    lead = 6.0
     early = {name: max(ready[name], issue[name] - lead) for name in msgs}
     return early, arrive
 
@@ -186,7 +186,7 @@
     events = [(issue[name], 0, i, ("send", name)) for i, name in enumerate(msgs)]
     at = 0.0
     for i, (when, need, dy, dx) in enumerate(tasks):
-        at = max(at, when)
+        at = max(at, when + (3.0 if dy != 2 else 0.0))
         events.append((at, 1, i, ("dot", need, dy, dx)))
         at += 1.3
     events.sort(key=lambda e: e[:3])
@@ -243,45 +243,37 @@
 
     ins = [(w_hbm, w_in), (tok_hbm, tok_in), (gain_hbm, gain), (mf_hbm, mf), (f_hbm, fmat), (g_hbm, gmat), (sf_hbm, sf), (skip_hbm, skip)]
     loads = [pltpu.make_async_copy(src, dst, local_sem.at[i]) for i, (src, dst) in enumerate(ins)]
-    for load in loads:
-        load.start()
+    for i in (1, 2, 0, 3, 4, 5, 6, 7):
+        loads[i].start()
 
     def dev(dy, ds, dz):
         return ((y + dy) % 4, ds, (z + dz) % 8)
 
     barrier = pltpu.get_barrier_semaphore()
-    peers = [dev(0, s, k) for k in range(1, 8)] + [dev(0, (s + k) % 8, 0) for k in range(1, 8)] + [dev(k, s, 0) for k in range(1, 4)]
+    peers = [dev(0, s, k) for k in range(1, 8)] + [dev(dy, (s + k) % 8, 0) for dy in range(4) for k in range(8) if dy or k]
     for peer in peers:
         pl.semaphore_signal(barrier, inc=1, device_id=peer, device_id_type=MESH)
 
-    loads[0].wait()
-    top = jnp.zeros((8, 512), F32)
-    part = [jnp.zeros((8, 512), F32) for _ in range(4)]
-    for k in range(3):
-        for r in range(0, 256, 32):
-            for j in range(4):
-                part[j] = jnp.maximum(part[j], jnp.abs(w_in[k, r + 8 * j : r + 8 * j + 8, :]))
-    top = jnp.maximum(jnp.maximum(part[0], part[1]), jnp.maximum(part[2], part[3]))
-    top = jnp.max(jnp.max(top, axis=0, keepdims=True), axis=1, keepdims=True)
-    peaks[0] = jnp.broadcast_to(top, (8, 128))
-
-    def norm_rows(lo):
-        for r in range(lo, lo + 32, 16):
-            v = tok_in[r : r + 16, :].astype(F32)
-            mean = jnp.sum(v * v, axis=1, keepdims=True) * F32(1.0 / 8192)
-            a_all[r : r + 16, :] = (v * lax.rsqrt(mean + F32(eps_norm)) * gain[...]).astype(BF16)
-
     loads[1].wait()
     loads[2].wait()
-    norm_rows(0)
-    norm_rows(32)
+    root = []
+    for r in range(0, 64, 16):
+        v = tok_in[r : r + 16, :].astype(F32)
+        root.append(lax.rsqrt(jnp.sum(v * v, axis=1, keepdims=True) * F32(1.0 / 8192) + F32(eps_norm)))
+
+    def norm_columns(dy):
+        cols = pl.ds(pl.multiple_of(((y + dy) % 4) * 2048, 2048), 2048)
+        for r in range(0, 64, 16):
+            a_all[r : r + 16, cols] = (tok_in[r : r + 16, cols].astype(F32) * root[r // 16] * gain[:, cols]).astype(BF16)
+
+    norm_columns(0)
 
     def peak_round(src, base, targets):
         copies = []
         for i, target in enumerate(targets):
             copies.append(
                 pltpu.make_async_remote_copy(
-                    src_ref=peaks.at[src], dst_ref=peaks.at[3 + base + i],
+                    src_ref=peaks.at[src], dst_ref=peaks.at[2 + base + i],
                     send_sem=pk_send.at[base + i], recv_sem=pk_recv.at[base + i],
                     device_id=target, device_id_type=MESH,
                 )
@@ -294,7 +286,7 @@
         best = peaks[src]
         for i, copy in enumerate(copies):
             copy.wait_recv()
-            best = jnp.maximum(best, peaks[3 + base + i])
+            best = jnp.maximum(best, peaks[2 + base + i])
         return best
 
     def w_row(dy, dx, parity):
@@ -344,14 +336,31 @@
                 copies[name].wait_recv()
 
     pl.semaphore_wait(barrier, len(peers))
+    for name in started[:2]:
+        copies[name].start()
+
+    loads[0].wait()
+    top = jnp.zeros((8, 512), F32)
+    part = [jnp.zeros((8, 512), F32) for _ in range(4)]
+    for k in range(3):
+        for r in range(0, 256, 32):
+            for j in range(4):
+                part[j] = jnp.maximum(part[j], jnp.abs(w_in[k, r + 8 * j : r + 8 * j + 8, :]))
+    top = jnp.maximum(jnp.maximum(part[0], part[1]), jnp.maximum(part[2], part[3]))
+    top = jnp.max(jnp.max(top, axis=0, keepdims=True), axis=1, keepdims=True)
+    peaks[0] = jnp.broadcast_to(top, (8, 128))
+
     round0 = peak_round(0, 0, peers[:7])
-    for name in started:
+    norm_columns(-1)
+    for name in started[2:4]:
         copies[name].start()
+    norm_columns(1)
+    for name in started[4:6]:
+        copies[name].start()
+    norm_columns(2)
     peaks[1] = peak_finish(round0, 0, 0)
-    round1 = peak_round(1, 7, peers[7:14])
-    peaks[2] = peak_finish(round1, 1, 7)
-    round2 = peak_round(2, 14, peers[14:])
-    peak = peak_finish(round2, 2, 14)
+    round1 = peak_round(1, 7, peers[7:])
+    peak = peak_finish(round1, 1, 7)
     peak_ref[0] = jnp.max(peak)
 
     ratio = F32(grid_top) / (peak + F32(eps_peak))
@@ -482,7 +491,7 @@
     mix(0)
     rim.wait_send()
     edge.wait_send()
-    for copy in round0 + round1 + round2:
+    for copy in round0 + round1:
         copy.wait_send()
     for copy in copies.values():
         copy.wait_send()
@@ -514,12 +523,12 @@
             pltpu.VMEM((520, 1536), F32),
             pltpu.VMEM((640, 512), BF16),
             pltpu.VMEM((3, 128, 512), F32),
-            pltpu.VMEM((20, 8, 128), F32),
+            pltpu.VMEM((40, 8, 128), F32),
             pltpu.SemaphoreType.DMA((8,)),
             pltpu.SemaphoreType.DMA((count,)),
             pltpu.SemaphoreType.DMA((count,)),
-            pltpu.SemaphoreType.DMA((17,)),
-            pltpu.SemaphoreType.DMA((17,)),
+            pltpu.SemaphoreType.DMA((38,)),
+            pltpu.SemaphoreType.DMA((38,)),
             pltpu.SemaphoreType.DMA((2,)),
             pltpu.SemaphoreType.DMA((2,)),
         ],

time: 109 us -> 115 us (1.055)
  Pallas kernels: 105 us -> 111 us
    pallas_call x1, Pallas kernels: 105 us -> 111 us  [shards(): pl.pallas_call(functools.partial(kernel, (msgs, events, ids)), out_shape=...]
where the time goes in v3:
time: 115 us
  Pallas kernels  111 us (97%)
  between operations  2.34 us (2%)
  local copies, waits for them, and re-layouts  1.87 us (2%)
    pallas_call x1, Pallas kernels, shards(): pl.pallas_call(functools.partial(kernel, (msgs, events, ids)), out_shape=...  111 us

profile of v3, /device:TPU:1, one launch (start us, length us, event | category | flops | bytes accessed | tf_op | source)
XLA Modules:
  0.0 115.1 jit_solution(5272504255693198676)
XLA Ops:
  0.6 110.9 %shard_map.95 = (bf16[512,512]{1,0:T(8,128)(2,1)}, f32[1]{0:T(128)}) custom-call(bf16[64,8192]{1,0:T(8,128)(2,1)} %bitcast.6, f32[1,8192]{1,0:T(1,128)} %bitcast.8, f32[3,256,512]{2,1,0:T(8,128)} %bitcast.5, f32[3,3,512]{2,1,0:T(4,128)} %sf_hbm.1, bf16[128,512]{1,0:T(8,128)(2,1)} %mf_hbm.1, f32[1,512]{1,0:T(1,128)} %bitcast.9, ...), custom_call_target="tpu_custom_call" | custom-call | tf_op jit(solution)/shard_map/pallas_call | solution.py:506
  111.5 1.9 %copy.12 = bf16[1,512,512]{2,1,0:T(8,128)(2,1)} copy(bf16[1,512,512]{2,1,0:T(8,128)(2,1)} %bitcast.7) | data formatting | bytes 1048576

commit v4 on v3

--- a/solution.py
+++ b/solution.py
@@ -163,7 +163,7 @@
         if not heap or heap[0][0] > now:
             for key in queue:
                 serve(key, now)
-    lead = 6.0
+    lead = 1.5
     early = {name: max(ready[name], issue[name] - lead) for name in msgs}
     return early, arrive
 
@@ -186,7 +186,7 @@
     events = [(issue[name], 0, i, ("send", name)) for i, name in enumerate(msgs)]
     at = 0.0
     for i, (when, need, dy, dx) in enumerate(tasks):
-        at = max(at, when + (3.0 if dy != 2 else 0.0))
+        at = max(at, when)
         events.append((at, 1, i, ("dot", need, dy, dx)))
         at += 1.3
     events.sort(key=lambda e: e[:3])

time: 115 us -> 116 us (level)
    pallas_call x1, Pallas kernels: 111 us -> 112 us  [shards(): pl.pallas_call(functools.partial(kernel, (msgs, events, ids)), out_shape=...]
where the time goes in v4:
time: 116 us
  Pallas kernels  112 us (97%)
  between operations  2.34 us (2%)
  local copies, waits for them, and re-layouts  1.87 us (2%)
    pallas_call x1, Pallas kernels, shards(): pl.pallas_call(functools.partial(kernel, (msgs, events, ids)), out_shape=...  112 us

profile of v4, /device:TPU:1, one launch (start us, length us, event | category | flops | bytes accessed | tf_op | source)
XLA Modules:
  0.0 116.3 jit_solution(2932157256647479106)
XLA Ops:
  0.6 112.1 %shard_map.95 = (bf16[512,512]{1,0:T(8,128)(2,1)}, f32[1]{0:T(128)}) custom-call(bf16[64,8192]{1,0:T(8,128)(2,1)} %bitcast.6, f32[1,8192]{1,0:T(1,128)} %bitcast.8, f32[3,256,512]{2,1,0:T(8,128)} %bitcast.5, f32[3,3,512]{2,1,0:T(4,128)} %sf_hbm.1, bf16[128,512]{1,0:T(8,128)(2,1)} %mf_hbm.1, f32[1,512]{1,0:T(1,128)} %bitcast.9, ...), custom_call_target="tpu_custom_call" | custom-call | tf_op jit(solution)/shard_map/pallas_call | solution.py:506
  112.7 1.9 %copy.12 = bf16[1,512,512]{2,1,0:T(8,128)(2,1)} copy(bf16[1,512,512]{2,1,0:T(8,128)(2,1)} %bitcast.7) | data formatting | bytes 1048576

commit v5 on v2

--- a/solution.py
+++ b/solution.py
@@ -163,7 +163,7 @@
         if not heap or heap[0][0] > now:
             for key in queue:
                 serve(key, now)
-    lead = 3.0
+    lead = 6.0
     early = {name: max(ready[name], issue[name] - lead) for name in msgs}
     return early, arrive
 
@@ -186,7 +186,7 @@
     events = [(issue[name], 0, i, ("send", name)) for i, name in enumerate(msgs)]
     at = 0.0
     for i, (when, need, dy, dx) in enumerate(tasks):
-        at = max(at, when)
+        at = max(at, when + (3.0 if dy != 2 else 0.0))
         events.append((at, 1, i, ("dot", need, dy, dx)))
         at += 1.3
     events.sort(key=lambda e: e[:3])

time: 109 us -> 110 us (level)
  no operation moved by 1% of the time
where the time goes in v5:
time: 110 us
  Pallas kernels  106 us (96%)
  between operations  2.34 us (2%)
  local copies, waits for them, and re-layouts  1.87 us (2%)
    pallas_call x1, Pallas kernels, shards(): pl.pallas_call(functools.partial(kernel, (msgs, events, ids)), out_shape=...  106 us

profile of v5, /device:TPU:1, one launch (start us, length us, event | category | flops | bytes accessed | tf_op | source)
XLA Modules:
  0.0 110.2 jit_solution(6412362674204177667)
XLA Ops:
  0.6 106.0 %shard_map.95 = (bf16[512,512]{1,0:T(8,128)(2,1)}, f32[1]{0:T(128)}) custom-call(bf16[64,8192]{1,0:T(8,128)(2,1)} %bitcast.6, f32[1,8192]{1,0:T(1,128)} %bitcast.8, f32[3,256,512]{2,1,0:T(8,128)} %bitcast.5, f32[3,3,512]{2,1,0:T(4,128)} %sf_hbm.1, bf16[128,512]{1,0:T(8,128)(2,1)} %mf_hbm.1, f32[1,512]{1,0:T(1,128)} %bitcast.9, ...), custom_call_target="tpu_custom_call" | custom-call | tf_op jit(solution)/shard_map/pallas_call | solution.py:497
  106.6 1.9 %copy.12 = bf16[1,512,512]{2,1,0:T(8,128)(2,1)} copy(bf16[1,512,512]{2,1,0:T(8,128)(2,1)} %bitcast.7) | data formatting | bytes 1048576
